TPU v7x, 32 devices: a whole 2x2x4 slice. The times are simulated.
32 devices in a mesh: band: 4 (over y, core), fft: 8 (over z, x).
Axes of the slice: x: 2, y: 2, z: 4, core: 2. Of those that a mesh axis runs over, the one named last changes fastest.
Arguments:
- start_bands: float32 [2, 8, 96, 9216], P(None, 'band', 'fft'), may hold values from -6 to 6
- potential: float32 [96, 96, 96], P(None, None, 'fft'), may hold values from -2 to 1
- half_height: int32 [96, 96], P('fft'), may hold values from -1 to 24, as said below
- lower_bound: float32 [1], replicated, may hold values from 1 to 2
- upper_bound: float32 [1], replicated, may hold values from 14 to 16
- fermi_level: float32 [1], replicated, may hold values from 0 to 2
Outputs:
- filtered_bands: float32 [2, 8, 96, 9216], P(None, 'band', 'fft')
- energies: float32 [8], P('band')
- band_energy: float32 [1], replicated
Inputs may be any that keep to these rules, and one draw needn't show every extreme that they name: Column (x, y) keeps exactly the wave vectors whose z frequency f has |f| <= half_height[x, y]; -1 marks an empty column; the column of x = y = 0 holds 24; every column whose x or y frequency exceeds 96/4 in magnitude is empty.
All inputs are finite; a program needn't handle non-finite values.
Results may differ from a plain program's by a relative error of at most 0.0003.
Values sent between devices are 32-bit elements; how exact they have to be, the bound alone decides.
No kernel may reach another device: no remote copies, remote signals or barrier semaphores. Data moves between devices by JAX's collectives and lax.ppermute only.
A program may use at most 128 MiB of HBM per device.

v0:
```python
import math
import jax
import jax.numpy as jnp
import numpy as np
from jax import lax
from jax.sharding import PartitionSpec as P

DEGREE = 3
KIN_MAX = 12.0
TEMPER = 0.5
HIGHEST = lax.Precision.HIGHEST


def frequency_of(positions, length):
    return jnp.where(positions < length // 2, positions, positions - length)


def dft_tables(row_positions, col_positions, length):
    rows_int = jnp.asarray(row_positions, dtype=jnp.int32)
    cols_int = jnp.asarray(col_positions, dtype=jnp.int32)
    angle = (
        2.0
        * math.pi
        / length
        * (rows_int[:, None] * cols_int[None, :] % length).astype(jnp.float32)
    )
    return (jnp.cos(angle), jnp.sin(angle))


def transform(real_part, imag_part, pattern, tables, parity):
    cosine, sine = tables
    real_cos = jnp.einsum(pattern, real_part, cosine, precision=HIGHEST)
    real_sin = jnp.einsum(pattern, real_part, sine, precision=HIGHEST)
    imag_cos = jnp.einsum(pattern, imag_part, cosine, precision=HIGHEST)
    imag_sin = jnp.einsum(pattern, imag_part, sine, precision=HIGHEST)
    return (real_cos - parity * imag_sin, parity * real_sin + imag_cos)


def pick_box(array, axis, quarter, length):
    lower = lax.slice_in_dim(array, 0, quarter + 1, axis=axis)
    upper = lax.slice_in_dim(array, length - quarter, length, axis=axis)
    return jnp.concatenate([lower, upper], axis=axis)


def place_box(array, axis, quarter, length):
    lower = lax.slice_in_dim(array, 0, quarter + 1, axis=axis)
    upper = lax.slice_in_dim(array, quarter + 1, 2 * quarter + 1, axis=axis)
    shape = list(array.shape)
    shape[axis] = length - 2 * quarter - 1
    middle = jnp.zeros(tuple(shape), jnp.float32)
    return jnp.concatenate([lower, middle, upper], axis=axis)


def packed_operator(field_real, field_imag, potential):
    length = field_real.shape[3]
    quarter = length // 4
    whole = np.arange(length)
    kept = np.concatenate([np.arange(quarter + 1), np.arange(length - quarter, length)])
    box_to_whole = dft_tables(kept, whole, length)
    whole_to_box = dft_tables(whole, kept, length)
    whole_to_whole = dft_tables(whole, whole, length)
    kept_real = pick_box(pick_box(field_real, 2, quarter, length), 3, quarter, length)
    kept_imag = pick_box(pick_box(field_imag, 2, quarter, length), 3, quarter, length)
    z_real, z_imag = transform(kept_real, kept_imag, "bxyk,kn->bxyn", box_to_whole, 1.0)
    x_real = pick_box(
        lax.all_to_all(z_real, "fft", split_axis=3, concat_axis=1, tiled=True), 1, quarter, length
    )
    x_imag = pick_box(
        lax.all_to_all(z_imag, "fft", split_axis=3, concat_axis=1, tiled=True), 1, quarter, length
    )
    lined_real, lined_imag = transform(x_real, x_imag, "bkyz,kn->bnyz", box_to_whole, 1.0)
    space_real, space_imag = transform(lined_real, lined_imag, "bxkz,kn->bxnz", box_to_whole, 1.0)
    space_real = space_real * potential
    space_imag = space_imag * potential
    ready_real, ready_imag = transform(space_real, space_imag, "bxkz,kn->bxnz", whole_to_box, -1.0)
    back_real, back_imag = transform(ready_real, ready_imag, "bkyz,kn->bnyz", whole_to_whole, -1.0)
    line_real = lax.all_to_all(back_real, "fft", split_axis=1, concat_axis=3, tiled=True)
    line_imag = lax.all_to_all(back_imag, "fft", split_axis=1, concat_axis=3, tiled=True)
    final_real, final_imag = transform(line_real, line_imag, "bxyk,kn->bxyn", whole_to_box, -1.0)
    final_real = place_box(place_box(final_real, 3, quarter, length), 2, quarter, length)
    final_imag = place_box(place_box(final_imag, 3, quarter, length), 2, quarter, length)
    return (final_real, final_imag)


def hamiltonian(field_real, field_imag, potential, inside, kinetic):
    length = field_real.shape[3]
    final_real, final_imag = packed_operator(field_real, field_imag, potential)
    scale = 1.0 / float(length**3)
    return (
        inside * (kinetic * field_real + scale * final_real),
        inside * (kinetic * field_imag + scale * final_imag),
    )


def rotation(gram_real, gram_imag, total_bands):
    embedded = jnp.block([[gram_real, -gram_imag], [gram_imag, gram_real]])
    factor = jnp.linalg.cholesky(embedded)
    selector = jnp.eye(2 * total_bands, total_bands, dtype=jnp.float32)
    inverse_cols = lax.linalg.triangular_solve(
        factor, selector, left_side=True, lower=True, transpose_a=True
    )
    return (inverse_cols[:total_bands], inverse_cols[total_bands:])


def correlation(real_rows, imag_rows, cells_total):
    gram_real = (
        jnp.dot(real_rows, real_rows.T, precision=HIGHEST)
        + jnp.dot(imag_rows, imag_rows.T, precision=HIGHEST)
    ) / cells_total
    gram_imag = (
        jnp.dot(real_rows, imag_rows.T, precision=HIGHEST)
        - jnp.dot(imag_rows, real_rows.T, precision=HIGHEST)
    ) / cells_total
    return (gram_real, gram_imag)


def local(start_bands, potential, half_height, lower_bound, upper_bound, fermi_level):
    band_block = start_bands.shape[1]
    x_cells = start_bands.shape[2]
    length = potential.shape[0]
    cells_total = float(length**3)
    offset = lax.axis_index("fft") * x_cells
    freq_all = frequency_of(jnp.arange(length, dtype=jnp.int32), length)
    freq_x = frequency_of(offset + jnp.arange(x_cells, dtype=jnp.int32), length)
    inside = (jnp.abs(freq_all)[None, None, :] <= half_height[:, :, None]).astype(jnp.float32)
    squared = (
        freq_x[:, None, None] ** 2 + freq_all[None, :, None] ** 2 + freq_all[None, None, :] ** 2
    )
    kinetic = KIN_MAX / (length // 4) ** 2 * squared.astype(jnp.float32)

    def apply_h(field):
        return jnp.stack(hamiltonian(field[0], field[1], potential, inside, kinetic))

    shaped = start_bands.reshape(2, band_block, x_cells, length, length)
    center = 0.5 * (upper_bound[0] + lower_bound[0])
    half_width = 0.5 * (upper_bound[0] - lower_bound[0])
    previous = inside * shaped
    current = (apply_h(previous) - center * previous) / half_width
    for degree_step in range(1, DEGREE):
        following = 2.0 * (apply_h(current) - center * current) / half_width - previous
        previous, current = (current, following)
    flattened = current.reshape(2, band_block, x_cells, length * length)
    everything = lax.all_gather(flattened, "band", axis=1, tiled=True)
    total_bands = everything.shape[1]
    real_rows = everything[0].reshape(total_bands, -1)
    imag_rows = everything[1].reshape(total_bands, -1)
    part_real, part_imag = correlation(real_rows, imag_rows, cells_total)
    gram_real, gram_imag = lax.psum((part_real, part_imag), "fft")
    upper_rows, lower_rows = rotation(gram_real, gram_imag, total_bands)
    first_band = lax.axis_index("band") * band_block
    upper_own = lax.dynamic_slice_in_dim(upper_rows, first_band, band_block, 1)
    lower_own = lax.dynamic_slice_in_dim(lower_rows, first_band, band_block, 1)
    rot_real = jnp.dot(upper_own.T, real_rows, precision=HIGHEST) - jnp.dot(
        lower_own.T, imag_rows, precision=HIGHEST
    )
    rot_imag = jnp.dot(upper_own.T, imag_rows, precision=HIGHEST) + jnp.dot(
        lower_own.T, real_rows, precision=HIGHEST
    )
    rotated_flat = jnp.stack([rot_real, rot_imag]).reshape(2, band_block, x_cells, length * length)
    rotated = rotated_flat.reshape(2, band_block, x_cells, length, length)
    applied = apply_h(rotated)
    partial_energy = jnp.sum(rotated * applied, axis=(0, 2, 3, 4)) / cells_total
    energies = lax.psum(partial_energy, "fft")
    weights = jax.nn.sigmoid((fermi_level[0] - energies) / TEMPER)
    weighted = jnp.sum(weights * energies)
    summed = lax.psum(weighted, "band")
    band_energy = (summed / float(band_block * lax.axis_size("band"))).reshape(1)
    return (rotated_flat, energies, band_energy)


def solution(mesh):
    placed = (P(None, "band", "fft", None), P(None, None, "fft"), P("fft", None), P(), P(), P())
    return jax.shard_map(
        local,
        mesh=mesh,
        in_specs=placed,
        out_specs=(P(None, "band", "fft", None), P("band"), P()),
        check_vma=False,
    )
```

profile of v0, /device:TPU:0, one launch (start us, length us, event | category | flops | bytes accessed | tf_op | source)
XLA Modules:
  0.0 820.1 jit_solution(6142604778680343717)
XLA Ops:
  23.6 7.3 all-to-all-start
  44.0 4.3 all-to-all-start.1
  107.6 6.2 all-to-all-start.2
  121.8 4.2 reshape.508
  126.0 6.0 all-to-all-start.3
  184.0 6.0 all-to-all-start.4
  196.5 4.2 reshape.512
  201.1 5.8 all-to-all-start.5
  260.6 4.2 reshape.514
  264.8 6.2 all-to-all-start.6
  277.1 4.2 reshape.516
  281.3 6.0 all-to-all-start.7
  336.6 6.0 all-to-all-start.8
  352.3 4.5 all-to-all-start.9
  393.9 4.2 reshape.522
  398.0 4.5 all-to-all-start.10
  412.2 4.9 all-to-all-start.11
  465.1 5.7 divide_subtract_fusion
  473.4 52.4 %all-gather.2.cloned.1.call-done = f32[2,8,12,9216]{3,0,2,1:T(2,128)} async-done(((f32[2,2,12,9216]{3,0,2,1:T(2,128)}), f32[2,8,12,9216]{3,0,2,1:T(2,128)}) %all-gather.2.cloned.1.call-update) | async-done | bytes 7077904 | tf_op jit(solution)/shard_map/all_gather | solution.py:143
  525.8 10.0 %fusion.1106 = (f32[1,8,12,9216]{3,0,2,1:T(1,128)S(1)}, f32[1,8,12,9216]{3,0,2,1:T(1,128)S(1)}) fusion(f32[2,8,12,9216]{3,0,2,1:T(2,128)} %all-gather.2.cloned.1.call-done), kind=kLoop, calls=%fused_computation.1039 | loop fusion | bytes 14155776 | tf_op jit(solution)/shard_map/slice | solution.py:145
  535.7 8.2 %fusion.78 = f32[8,8]{0,1:T(8,128)S(1)} fusion(f32[1,8,12,9216]{3,0,2,1:T(1,128)S(1)} %get-tuple-element.14), kind=kOutput, calls=%fused_computation.172 | convolution fusion | flops 84934656 | bytes 3539200 | tf_op jit(solution)/shard_map/dot_general | solution.py:107
  543.9 10.0 %fusion.84 = f32[8,8]{0,1:T(8,128)S(1)} fusion(f32[1,8,12,9216]{3,0,2,1:T(1,128)S(1)} %get-tuple-element.15, f32[1,8,12,9216]{3,0,2,1:T(1,128)S(1)} %get-tuple-element.14), kind=kOutput, calls=%fused_computation.174 | convolution fusion | flops 84934656 | bytes 7078144 | tf_op jit(solution)/shard_map/dot_general | solution.py:111
  561.7 10.0 %fusion.105 = f32[8,8]{0,1:T(8,128)S(1)} fusion(f32[8,8]{0,1:T(8,128)S(1)} %fusion.84, f32[1,8,12,9216]{3,0,2,1:T(1,128)S(1)} %get-tuple-element.15, f32[1,8,12,9216]{3,0,2,1:T(1,128)S(1)} %get-tuple-element.14), kind=kOutput, calls=%fused_computation.179 | convolution fusion | flops 84934784 | bytes 7078400 | tf_op jit(solution)/shard_map/dot_general | solution.py:112
  571.7 8.4 %fusion.97 = f32[8,8]{0,1:T(8,128)S(1)} fusion(f32[8,8]{0,1:T(8,128)S(1)} %fusion.78, f32[1,8,12,9216]{3,0,2,1:T(1,128)S(1)} %get-tuple-element.15), kind=kOutput, calls=%fused_computation.177 | convolution fusion | flops 84934784 | bytes 3539456 | tf_op jit(solution)/shard_map/dot_general | solution.py:108
  580.1 22.0 %all-reduce = (f32[8,8]{0,1:T(8,128)S(1)}, f32[8,8]{0,1:T(8,128)S(1)}) all-reduce(f32[8,8]{0,1:T(8,128)S(1)} %fusion.97, f32[8,8]{0,1:T(8,128)S(1)} %fusion.105), channel_id=1, replica_groups=mesh['band'=4,'fft'=8] {'fft'}, use_global_device_ids=true, to_apply=%region_0.1 | all-reduce | flops 128 | bytes 1024 | tf_op jit(solution)/shard_map/psum | solution.py:148
  606.7 5.3 fusion.752
  620.8 5.3 fusion.754
  659.8 6.1 all-to-all-start.13
  723.4 6.2 all-to-all-start.14
  740.0 6.0 all-to-all-start.15
  779.7 21.8 %psum.30 = f32[2]{0:T(128)S(1)} all-reduce(f32[2]{0:T(128)S(1)} %broadcast_multiply_fusion), channel_id=1, replica_groups=mesh['band'=4,'fft'=8] {'fft'}, use_global_device_ids=true, to_apply=%region_5.6 | all-reduce | flops 2 | bytes 16 | tf_op jit(solution)/shard_map/psum | solution.py:163
  804.7 6.5 psum.31
  (549 shorter events, 527.1 us)
Async XLA Ops:
  23.6 20.4 %all-to-all-start = ((f32[8,1,14112]{2,1,0:T(1,128)}), f32[8,1,14112]{2,1,0:T(1,128)}, u32[]{:S(2)}, u32[]{:S(2)}) async-start(f32[8,1,14112]{2,1,0:T(1,128)} %reshape.502), calls=%async_computation | async-start | bytes 909312 | tf_op jit(solution)/shard_map/all_to_all | solution.py:66
  44.0 16.9 %all-to-all-start.1 = ((f32[8,1,14112]{2,1,0:T(1,128)}), f32[8,1,14112]{2,1,0:T(1,128)}, u32[]{:S(2)}, u32[]{:S(2)}) async-start(f32[8,1,14112]{2,1,0:T(1,128)} %reshape.504), calls=%async_computation.1 | async-start | bytes 909312 | tf_op jit(solution)/shard_map/all_to_all | solution.py:69
  75.7 3.2 copy-start.60
  75.7 3.2 copy-start.63
  107.6 18.4 %all-to-all-start.2 = ((f32[8,1,14112]{2,1,0:T(1,128)}), f32[8,1,14112]{2,1,0:T(1,128)}, u32[]{:S(2)}, u32[]{:S(2)}) async-start(f32[8,1,14112]{2,1,0:T(1,128)} %reshape.506), calls=%async_computation.2 | async-start | bytes 909312 | tf_op jit(solution)/shard_map/all_to_all | solution.py:77
  126.0 23.4 %all-to-all-start.3 = ((f32[8,1,14112]{2,1,0:T(1,128)}), f32[8,1,14112]{2,1,0:T(1,128)}, u32[]{:S(2)}, u32[]{:S(2)}) async-start(f32[8,1,14112]{2,1,0:T(1,128)} %reshape.508), calls=%async_computation.3 | async-start | bytes 909312 | tf_op jit(solution)/shard_map/all_to_all | solution.py:78
  184.0 17.1 %all-to-all-start.4 = ((f32[8,1,14112]{2,1,0:T(1,128)}), f32[8,1,14112]{2,1,0:T(1,128)}, u32[]{:S(2)}, u32[]{:S(2)}) async-start(f32[8,1,14112]{2,1,0:T(1,128)} %reshape.510), calls=%async_computation.4 | async-start | bytes 909312 | tf_op jit(solution)/shard_map/all_to_all | solution.py:66
  201.1 16.5 %all-to-all-start.5 = ((f32[8,1,14112]{2,1,0:T(1,128)}), f32[8,1,14112]{2,1,0:T(1,128)}, u32[]{:S(2)}, u32[]{:S(2)}) async-start(f32[8,1,14112]{2,1,0:T(1,128)} %reshape.512), calls=%async_computation.5 | async-start | bytes 909312 | tf_op jit(solution)/shard_map/all_to_all | solution.py:69
  232.4 3.2 copy-start.61
  232.4 3.2 copy-start.64
  264.8 16.6 %all-to-all-start.6 = ((f32[8,1,14112]{2,1,0:T(1,128)}), f32[8,1,14112]{2,1,0:T(1,128)}, u32[]{:S(2)}, u32[]{:S(2)}) async-start(f32[8,1,14112]{2,1,0:T(1,128)} %reshape.514), calls=%async_computation.6 | async-start | bytes 909312 | tf_op jit(solution)/shard_map/all_to_all | solution.py:77
  281.3 21.1 %all-to-all-start.7 = ((f32[8,1,14112]{2,1,0:T(1,128)}), f32[8,1,14112]{2,1,0:T(1,128)}, u32[]{:S(2)}, u32[]{:S(2)}) async-start(f32[8,1,14112]{2,1,0:T(1,128)} %reshape.516), calls=%async_computation.7 | async-start | bytes 909312 | tf_op jit(solution)/shard_map/all_to_all | solution.py:78
  336.6 15.7 %all-to-all-start.8 = ((f32[8,1,14112]{2,1,0:T(1,128)}), f32[8,1,14112]{2,1,0:T(1,128)}, u32[]{:S(2)}, u32[]{:S(2)}) async-start(f32[8,1,14112]{2,1,0:T(1,128)} %reshape.518), calls=%async_computation.8 | async-start | bytes 909312 | tf_op jit(solution)/shard_map/all_to_all | solution.py:66
  352.3 13.8 %all-to-all-start.9 = ((f32[8,1,14112]{2,1,0:T(1,128)}), f32[8,1,14112]{2,1,0:T(1,128)}, u32[]{:S(2)}, u32[]{:S(2)}) async-start(f32[8,1,14112]{2,1,0:T(1,128)} %reshape.520), calls=%async_computation.9 | async-start | bytes 909312 | tf_op jit(solution)/shard_map/all_to_all | solution.py:69
  393.9 8.7 %copy-start.100 = (s32[96]{0:T(128)S(1)}, s32[96]{0:T(128)}, u32[]{:S(2)}) copy-start(s32[96]{0:T(128)} %copy-done.99) | copy-start | bytes 1156
  398.0 14.2 %all-to-all-start.10 = ((f32[8,1,14112]{2,1,0:T(1,128)}), f32[8,1,14112]{2,1,0:T(1,128)}, u32[]{:S(2)}, u32[]{:S(2)}) async-start(f32[8,1,14112]{2,1,0:T(1,128)} %reshape.522), calls=%async_computation.10 | async-start | bytes 909312 | tf_op jit(solution)/shard_map/all_to_all | solution.py:77
  406.7 10.5 %copy-start.93 = (s32[12,9216]{1,0:T(8,128)S(1)}, s32[12,9216]{1,0:T(8,128)}, u32[]{:S(2)}) copy-start(s32[12,9216]{1,0:T(8,128)} %le.38) | copy-start | bytes 1327108
  409.7 8.4 %copy-start.13 = (f32[1,2,12,96,96]{4,3,2,1,0:T(8,128)S(1)}, f32[1,2,12,96,96]{4,3,2,1,0:T(8,128)}, u32[]{:S(2)}) copy-start(f32[1,2,12,96,96]{4,3,2,1,0:T(8,128)} %copy-done.11) | copy-start | bytes 2654212
  412.2 28.9 %all-to-all-start.11 = ((f32[8,1,14112]{2,1,0:T(1,128)}), f32[8,1,14112]{2,1,0:T(1,128)}, u32[]{:S(2)}, u32[]{:S(2)}) async-start(f32[8,1,14112]{2,1,0:T(1,128)} %reshape.524), calls=%async_computation.11 | async-start | bytes 909312 | tf_op jit(solution)/shard_map/all_to_all | solution.py:78
  417.2 108.6 %all-gather.2.cloned.1.call-start = ((), (), s32[]{:S(2)}) async-start(), calls=%async_computation.16 | async-start | bytes 8847360 | tf_op jit(solution)/shard_map/all_gather | solution.py:143
  461.3 3.8 copy-start.92
  606.7 5.3 copy-start.1
  620.8 5.3 copy-start
  632.6 3.1 copy-start.25
  645.0 14.9 %all-to-all-start.12 = ((f32[8,1,14112]{2,1,0:T(1,128)}), f32[8,1,14112]{2,1,0:T(1,128)}, u32[]{:S(2)}, u32[]{:S(2)}) async-start(f32[8,1,14112]{2,1,0:T(1,128)} %reshape.526), calls=%async_computation.12 | async-start | bytes 909312 | tf_op jit(solution)/shard_map/all_to_all | solution.py:66
  659.8 16.7 %all-to-all-start.13 = ((f32[8,1,14112]{2,1,0:T(1,128)}), f32[8,1,14112]{2,1,0:T(1,128)}, u32[]{:S(2)}, u32[]{:S(2)}) async-start(f32[8,1,14112]{2,1,0:T(1,128)} %reshape.528), calls=%async_computation.13 | async-start | bytes 909312 | tf_op jit(solution)/shard_map/all_to_all | solution.py:69
  691.3 3.2 copy-start.62
  691.4 3.2 copy-start.65
  723.4 16.6 %all-to-all-start.14 = ((f32[8,1,14112]{2,1,0:T(1,128)}), f32[8,1,14112]{2,1,0:T(1,128)S(1)}, u32[]{:S(2)}, u32[]{:S(2)}) async-start(f32[8,1,14112]{2,1,0:T(1,128)} %reshape.530), calls=%async_computation.14 | async-start | bytes 909312 | tf_op jit(solution)/shard_map/all_to_all | solution.py:77
  740.0 8.5 %copy-start.94 = (f32[8,1,14112]{2,1,0:T(1,128)}, f32[8,1,14112]{2,1,0:T(1,128)S(1)}, u32[]{:S(2)}) copy-start(f32[8,1,14112]{2,1,0:T(1,128)S(1)} %all-to-all-done.14) | copy-start | bytes 1354756
  740.0 22.0 %all-to-all-start.15 = ((f32[8,1,14112]{2,1,0:T(1,128)}), f32[8,1,14112]{2,1,0:T(1,128)}, u32[]{:S(2)}, u32[]{:S(2)}) async-start(f32[8,1,14112]{2,1,0:T(1,128)} %reshape.532), calls=%async_computation.15 | async-start | bytes 909312 | tf_op jit(solution)/shard_map/all_to_all | solution.py:78
  801.5 3.2 copy-start.101
  (87 other events, 151.3 us)
Sparse Core Ops, SparseCore 0:
  473.5 52.2 all-gather.1
where the time goes:
time: 834 us; the launch traced here: 820 us
  local copies, waits for them, and re-layouts  328 us (39%)
  matrix products  194 us (23%)
  starting transfers between devices  90.2 us (11%)
  other arithmetic  73.5 us (9%)
  waiting for transfers between devices  63.7 us (8%)
  blocking collectives  50.4 us (6%)
  between operations  20.3 us (2%)
    unnamed x256, local copies, waits for them, and re-layouts  181 us
    all_gather x1, waiting for transfers between devices, local(): everything = lax.all_gather(flattened, 'band', axis=1, tiled=True)  52.4 us
    dot_general x24, matrix products, transform(): real_sin = jnp.einsum(pattern, real_part, sine, precision=HIGHEST)  44.5 us
    dot_general x24, matrix products, transform(): imag_sin = jnp.einsum(pattern, imag_part, sine, precision=HIGHEST)  35.1 us
    dot_general x24, matrix products, transform(): imag_cos = jnp.einsum(pattern, imag_part, cosine, precision=HIGHEST)  30.3 us
    dot_general x24, matrix products, transform(): real_cos = jnp.einsum(pattern, real_part, cosine, precision=HIGHEST)  29.4 us
    all_to_all x4, starting transfers between devices, packed_operator(): lax.all_to_all(z_real, 'fft', split_axis=3, concat_axis=1, tiled=True)  23.4 us
    all_to_all x4, starting transfers between devices, packed_operator(): lax.all_to_all(back_real, 'fft', split_axis=1, concat_axis=3, tiled=True)  23.1 us
  transfers between devices with their start and end apart: 17, of which 7 were waited for; matrix products, arithmetic and copies ran while one was open for 23% of the time, Pallas kernels for 0%

commit v1 on v0

--- a/solution.py
+++ b/solution.py
@@ -140,7 +140,8 @@
         following = 2.0 * (apply_h(current) - center * current) / half_width - previous
         previous, current = (current, following)
     flattened = current.reshape(2, band_block, x_cells, length * length)
-    everything = lax.all_gather(flattened, "band", axis=1, tiled=True)
+    tiles = lax.all_gather(flattened, "band")
+    everything = jnp.concatenate(tiles, axis=1)
     total_bands = everything.shape[1]
     real_rows = everything[0].reshape(total_bands, -1)
     imag_rows = everything[1].reshape(total_bands, -1)

time: 834 us -> 786 us (0.942)
  local copies, waits for them, and re-layouts: 328 us -> 286 us
  matrix products: 194 us -> 178 us
  waiting for transfers between devices: 63.7 us -> 78.5 us
    unnamed x256 -> x240, local copies, waits for them, and re-layouts: 181 us -> 161 us
    slice x1, local copies, waits for them, and re-layouts: 9.97 us -> 1.01 us  [local(): real_rows = everything[0].reshape(total_bands, -1)]
  transfers between devices with their start and end apart: 17 -> 17, of which waited for: 7 -> 10; matrix products, arithmetic and copies ran while one was open for 23% -> 22% of each run, Pallas kernels for 0% -> 0%
where the time goes in v1:
time: 786 us; the launch traced here: 773 us
  local copies, waits for them, and re-layouts  286 us (36%)
  matrix products  178 us (23%)
  starting transfers between devices  83.9 us (11%)
  waiting for transfers between devices  78.5 us (10%)
  other arithmetic  74.5 us (9%)
  blocking collectives  50.6 us (6%)
  between operations  20.7 us (3%)
    unnamed x240, local copies, waits for them, and re-layouts  161 us
    all_gather x1, waiting for transfers between devices, local(): tiles = lax.all_gather(flattened, 'band')  52.4 us
    dot_general x24, matrix products, transform(): real_sin = jnp.einsum(pattern, real_part, sine, precision=HIGHEST)  39.6 us
    dot_general x24, matrix products, transform(): imag_sin = jnp.einsum(pattern, imag_part, sine, precision=HIGHEST)  32.6 us
    dot_general x24, matrix products, transform(): real_cos = jnp.einsum(pattern, real_part, cosine, precision=HIGHEST)  28.5 us
    dot_general x24, matrix products, transform(): imag_cos = jnp.einsum(pattern, imag_part, cosine, precision=HIGHEST)  28.2 us
    all_to_all x4, starting transfers between devices, packed_operator(): lax.all_to_all(z_real, 'fft', split_axis=3, concat_axis=1, tiled=True)  23.4 us
    psum x1, blocking collectives, local(): gram_real, gram_imag = lax.psum((part_real, part_imag), 'fft')  22.3 us
  transfers between devices with their start and end apart: 17, of which 10 were waited for; matrix products, arithmetic and copies ran while one was open for 22% of the time, Pallas kernels for 0%

profile of v1, /device:TPU:0, one launch (start us, length us, event | category | flops | bytes accessed | tf_op | source)
XLA Modules:
  0.0 772.6 jit_solution(5706729185562711395)
XLA Ops:
  19.5 4.2 reshape.520
  23.7 7.3 all-to-all-start
  44.1 4.3 all-to-all-start.1
  103.7 4.2 reshape.524
  107.9 6.0 all-to-all-start.2
  121.9 4.2 reshape.526
  126.1 6.0 all-to-all-start.3
  179.9 4.2 reshape.528
  184.1 6.0 all-to-all-start.4
  201.2 5.9 all-to-all-start.5
  264.6 6.3 all-to-all-start.6
  277.1 4.2 reshape.534
  281.3 6.0 all-to-all-start.7
  336.5 6.0 all-to-all-start.8
  352.2 4.3 all-to-all-start.9
  398.0 4.5 all-to-all-start.10
  412.2 5.0 all-to-all-start.11
  460.6 6.8 divide_subtract_fusion
  467.4 52.4 %all-gather.3.cloned.1.call-done = f32[8,2,12,9216]{3,1,2,0:T(2,128)} async-done(((f32[2,2,12,9216]{3,1,2,0:T(2,128)}), f32[8,2,12,9216]{3,1,2,0:T(2,128)}) %all-gather.3.cloned.1.call-update) | async-done | bytes 7077904 | tf_op jit(solution)/shard_map/all_gather | solution.py:143
  519.8 5.3 copy.533
  530.2 7.6 fusion.1062
  537.9 8.1 %fusion.1063 = f32[8,8]{0,1:T(8,128)S(1)} fusion(f32[8,110592]{1,0:T(8,128)S(1)} %bitcast.558, f32[8,110592]{1,0:T(8,128)S(1)} %bitcast.552), kind=kOutput, calls=%fused_computation.1023 | convolution fusion | flops 84934656 | bytes 7078144 | tf_op jit(solution)/shard_map/dot_general | solution.py:111
  546.0 8.3 %fusion.68 = f32[8,8]{0,1:T(8,128)} fusion(f32[8,8]{0,1:T(8,128)S(1)} %fusion.1063, f32[8,110592]{1,0:T(8,128)S(1)} %bitcast.553, f32[8,110592]{1,0:T(8,128)S(1)} %bitcast.559), kind=kOutput, calls=%fused_computation.164 | convolution fusion | flops 84934784 | bytes 7078400 | tf_op jit(solution)/shard_map/dot_general | solution.py:112
  554.3 8.6 %fusion.69 = f32[8,8]{0,1:T(8,128)} fusion(f32[8,8]{0,1:T(8,128)S(1)} %fusion.1062, f32[8,110592]{1,0:T(8,128)S(1)} %bitcast.554), kind=kOutput, calls=%fused_computation.166 | convolution fusion | flops 84934784 | bytes 3539456 | tf_op jit(solution)/shard_map/dot_general | solution.py:108
  563.0 22.3 %all-reduce = (f32[8,8]{0,1:T(8,128)}, f32[8,8]{0,1:T(8,128)S(1)}) all-reduce(f32[8,8]{0,1:T(8,128)} %fusion.69, f32[8,8]{0,1:T(8,128)S(1)} %copy-done.90), channel_id=1, replica_groups=mesh['band'=4,'fft'=8] {'fft'}, use_global_device_ids=true, to_apply=%region_0.1 | all-reduce | flops 128 | bytes 1024 | tf_op jit(solution)/shard_map/psum | solution.py:149
  598.9 4.3 convolution_add_fusion
  609.7 5.1 fusion.714
  624.7 4.2 reshape.544
  638.7 4.3 all-to-all-done.12
  691.2 6.1 all-to-all-done.14
  732.0 21.8 %psum.30 = f32[2]{0:T(128)S(1)} all-reduce(f32[2]{0:T(128)S(1)} %broadcast_multiply_fusion), channel_id=1, replica_groups=mesh['band'=4,'fft'=8] {'fft'}, use_global_device_ids=true, to_apply=%region_5.6 | all-reduce | flops 2 | bytes 16 | tf_op jit(solution)/shard_map/psum | solution.py:164
  757.0 6.6 psum.31
  (533 shorter events, 491.6 us)
Async XLA Ops:
  10.2 441.4 %copy-start.4 = (f32[12,96,96]{2,1,0:T(8,128)}, f32[12,96,96]{2,1,0:T(8,128)S(1)}, u32[]{:S(2)}) copy-start(f32[12,96,96]{2,1,0:T(8,128)S(1)} %compare_convert_fusion.1) | copy-start | bytes 1327108
  23.7 20.4 %all-to-all-start = ((f32[8,1,14112]{2,1,0:T(1,128)}), f32[8,1,14112]{2,1,0:T(1,128)}, u32[]{:S(2)}, u32[]{:S(2)}) async-start(f32[8,1,14112]{2,1,0:T(1,128)} %reshape.520), calls=%async_computation | async-start | bytes 909312 | tf_op jit(solution)/shard_map/all_to_all | solution.py:66
  44.1 16.9 %all-to-all-start.1 = ((f32[8,1,14112]{2,1,0:T(1,128)}), f32[8,1,14112]{2,1,0:T(1,128)}, u32[]{:S(2)}, u32[]{:S(2)}) async-start(f32[8,1,14112]{2,1,0:T(1,128)} %reshape.522), calls=%async_computation.1 | async-start | bytes 909312 | tf_op jit(solution)/shard_map/all_to_all | solution.py:69
  49.7 337.7 %copy-start.2 = (f32[96,96,12]{0,1,2:T(8,128)}, f32[96,96,12]{0,1,2:T(8,128)S(1)}, u32[]{:S(2)}) copy-start(f32[96,96,12]{0,1,2:T(8,128)S(1)} %copy.345) | copy-start | bytes 1327108
  75.8 3.2 copy-start.56
  75.8 3.2 copy-start.58
  107.9 18.2 %all-to-all-start.2 = ((f32[8,1,14112]{2,1,0:T(1,128)}), f32[8,1,14112]{2,1,0:T(1,128)}, u32[]{:S(2)}, u32[]{:S(2)}) async-start(f32[8,1,14112]{2,1,0:T(1,128)} %reshape.524), calls=%async_computation.2 | async-start | bytes 909312 | tf_op jit(solution)/shard_map/all_to_all | solution.py:77
  126.1 23.4 %all-to-all-start.3 = ((f32[8,1,14112]{2,1,0:T(1,128)}), f32[8,1,14112]{2,1,0:T(1,128)}, u32[]{:S(2)}, u32[]{:S(2)}) async-start(f32[8,1,14112]{2,1,0:T(1,128)} %reshape.526), calls=%async_computation.3 | async-start | bytes 909312 | tf_op jit(solution)/shard_map/all_to_all | solution.py:78
  184.1 17.1 %all-to-all-start.4 = ((f32[8,1,14112]{2,1,0:T(1,128)}), f32[8,1,14112]{2,1,0:T(1,128)}, u32[]{:S(2)}, u32[]{:S(2)}) async-start(f32[8,1,14112]{2,1,0:T(1,128)} %reshape.528), calls=%async_computation.4 | async-start | bytes 909312 | tf_op jit(solution)/shard_map/all_to_all | solution.py:66
  201.2 16.5 %all-to-all-start.5 = ((f32[8,1,14112]{2,1,0:T(1,128)}), f32[8,1,14112]{2,1,0:T(1,128)}, u32[]{:S(2)}, u32[]{:S(2)}) async-start(f32[8,1,14112]{2,1,0:T(1,128)} %reshape.530), calls=%async_computation.5 | async-start | bytes 909312 | tf_op jit(solution)/shard_map/all_to_all | solution.py:69
  232.6 3.2 copy-start.57
  232.6 3.2 copy-start.59
  264.6 16.7 %all-to-all-start.6 = ((f32[8,1,14112]{2,1,0:T(1,128)}), f32[8,1,14112]{2,1,0:T(1,128)}, u32[]{:S(2)}, u32[]{:S(2)}) async-start(f32[8,1,14112]{2,1,0:T(1,128)} %reshape.532), calls=%async_computation.6 | async-start | bytes 909312 | tf_op jit(solution)/shard_map/all_to_all | solution.py:77
  281.3 20.9 %all-to-all-start.7 = ((f32[8,1,14112]{2,1,0:T(1,128)}), f32[8,1,14112]{2,1,0:T(1,128)}, u32[]{:S(2)}, u32[]{:S(2)}) async-start(f32[8,1,14112]{2,1,0:T(1,128)} %reshape.534), calls=%async_computation.7 | async-start | bytes 909312 | tf_op jit(solution)/shard_map/all_to_all | solution.py:78
  336.5 15.7 %all-to-all-start.8 = ((f32[8,1,14112]{2,1,0:T(1,128)}), f32[8,1,14112]{2,1,0:T(1,128)}, u32[]{:S(2)}, u32[]{:S(2)}) async-start(f32[8,1,14112]{2,1,0:T(1,128)} %reshape.536), calls=%async_computation.8 | async-start | bytes 909312 | tf_op jit(solution)/shard_map/all_to_all | solution.py:66
  352.2 13.8 %all-to-all-start.9 = ((f32[8,1,14112]{2,1,0:T(1,128)}), f32[8,1,14112]{2,1,0:T(1,128)}, u32[]{:S(2)}, u32[]{:S(2)}) async-start(f32[8,1,14112]{2,1,0:T(1,128)} %reshape.538), calls=%async_computation.9 | async-start | bytes 909312 | tf_op jit(solution)/shard_map/all_to_all | solution.py:69
  375.0 3.1 copy-start.87
  395.1 7.5 copy-start.92
  398.0 14.2 %all-to-all-start.10 = ((f32[8,1,14112]{2,1,0:T(1,128)}), f32[8,1,14112]{2,1,0:T(1,128)}, u32[]{:S(2)}, u32[]{:S(2)}) async-start(f32[8,1,14112]{2,1,0:T(1,128)} %reshape.540), calls=%async_computation.10 | async-start | bytes 909312 | tf_op jit(solution)/shard_map/all_to_all | solution.py:77
  406.7 10.5 %copy-start.84 = (s32[12,9216]{1,0:T(8,128)S(1)}, s32[12,9216]{1,0:T(8,128)}, u32[]{:S(2)}) copy-start(s32[12,9216]{1,0:T(8,128)} %le.38) | copy-start | bytes 1327108
  409.7 8.5 %copy-start.17 = (f32[1,2,12,96,96]{4,3,2,1,0:T(8,128)S(1)}, f32[1,2,12,96,96]{4,3,2,1,0:T(8,128)}, u32[]{:S(2)}) copy-start(f32[1,2,12,96,96]{4,3,2,1,0:T(8,128)} %copy-done.15) | copy-start | bytes 2654212
  412.2 28.9 %all-to-all-start.11 = ((f32[8,1,14112]{2,1,0:T(1,128)}), f32[8,1,14112]{2,1,0:T(1,128)S(1)}, u32[]{:S(2)}, u32[]{:S(2)}) async-start(f32[8,1,14112]{2,1,0:T(1,128)} %reshape.542), calls=%async_computation.11 | async-start | bytes 909312 | tf_op jit(solution)/shard_map/all_to_all | solution.py:78
  417.2 102.6 %all-gather.3.cloned.1.call-start = ((), (), s32[]{:S(2)}) async-start(), calls=%async_computation.16 | async-start | bytes 8847360 | tf_op jit(solution)/shard_map/all_gather | solution.py:143
  528.1 17.8 %copy-start = (f32[1,8,12,9216]{3,1,2,0:T(8,128)}, f32[1,8,12,9216]{3,1,2,0:T(8,128)S(1)}, u32[]{:S(2)}) copy-start(f32[1,8,12,9216]{3,1,2,0:T(8,128)S(1)} %copy.525) | copy-start | bytes 10616836
  554.3 8.6 %copy-start.90 = (f32[8,8]{0,1:T(8,128)S(1)}, f32[8,8]{0,1:T(8,128)}, u32[]{:S(2)}) copy-start(f32[8,8]{0,1:T(8,128)} %fusion.68) | copy-start | bytes 772
  595.7 3.2 copy-start.1
  628.9 14.1 %all-to-all-start.12 = ((f32[8,1,14112]{2,1,0:T(1,128)}), f32[8,1,14112]{2,1,0:T(1,128)}, u32[]{:S(2)}, u32[]{:S(2)}) async-start(f32[8,1,14112]{2,1,0:T(1,128)} %reshape.544), calls=%async_computation.12 | async-start | bytes 909312 | tf_op jit(solution)/shard_map/all_to_all | solution.py:66
  643.0 14.1 %all-to-all-start.13 = ((f32[8,1,14112]{2,1,0:T(1,128)}), f32[8,1,14112]{2,1,0:T(1,128)S(1)}, u32[]{:S(2)}, u32[]{:S(2)}) async-start(f32[8,1,14112]{2,1,0:T(1,128)} %reshape.546), calls=%async_computation.13 | async-start | bytes 909312 | tf_op jit(solution)/shard_map/all_to_all | solution.py:69
  681.7 15.6 %all-to-all-start.14 = ((f32[8,1,14112]{2,1,0:T(1,128)}), f32[8,1,14112]{2,1,0:T(1,128)S(1)}, u32[]{:S(2)}, u32[]{:S(2)}) async-start(f32[8,1,14112]{2,1,0:T(1,128)} %reshape.548), calls=%async_computation.14 | async-start | bytes 909312 | tf_op jit(solution)/shard_map/all_to_all | solution.py:77
  688.3 13.9 %copy-start.23 = (f32[2,110592]{1,0:T(2,128)S(1)}, f32[2,110592]{1,0:T(2,128)}, u32[]{:S(2)}) copy-start(f32[2,110592]{1,0:T(2,128)} %convolution_subtract_fusion) | copy-start | bytes 2654212
  697.4 19.5 %all-to-all-start.15 = ((f32[8,1,14112]{2,1,0:T(1,128)}), f32[8,1,14112]{2,1,0:T(1,128)}, u32[]{:S(2)}, u32[]{:S(2)}) async-start(f32[8,1,14112]{2,1,0:T(1,128)} %reshape.550), calls=%async_computation.15 | async-start | bytes 909312 | tf_op jit(solution)/shard_map/all_to_all | solution.py:78
  753.8 3.2 copy-start.93
  (79 other events, 132.5 us)
Sparse Core Ops, SparseCore 0:
  467.5 52.2 all-gather.2
